TPU v7x, 512 devices: a whole 4x4x16 slice. The times are simulated.
512 devices in a mesh: db: 16 (over y_hi, x, core), pb: 32 (over y_lo, z).
Axes of the slice: x: 4, y: 4 (y_hi: 2, y_lo: 2; y = y_hi * 2 + y_lo), z: 16, core: 2. Of those that a mesh axis runs over, the one named last changes fastest.
Arguments:
- queries: bfloat16 [8192, 768], P(('db', 'pb')), may hold values from -14 to 14
- passage_codes: int32 [65536, 64], P(('db', 'pb')), may hold values from 0 to 255
- codebooks: bfloat16 [64, 12, 256], replicated, may hold values from -4 to 4
- positives: int32 [8192], P(('db', 'pb')), may hold values from 0 to 2047
- loss_weight: float32 [8192], P(('db', 'pb')), may hold values from -12 to 12
Outputs:
- query_loss: float32 [8192], P(('db', 'pb'))
- grad_queries: float32 [8192, 768], P(('db', 'pb'))
- grad_codebooks: float32 [64, 12, 256], replicated
All inputs are finite; a program needn't handle non-finite values.
Results may differ from a plain program's by a relative error of at most 0.0055.
Values may be sent and summed in bfloat16 or wider, within the bound.
No kernel may reach another device: no remote copies, remote signals or barrier semaphores. Data moves between devices by JAX's collectives and lax.ppermute only.
A program may use at most 64 MiB of HBM per device.

v0:
```python
import math
import jax
import jax.numpy as jnp
from jax import lax
from jax.sharding import PartitionSpec as P


def shifted(block, axis, distance):
    devices = range(lax.axis_size(axis))
    route = [((i - distance) % len(devices), i) for i in devices]
    return lax.ppermute(block, axis, route)


def code_table(code_rows, level_count):
    levels = jnp.arange(level_count, dtype=jnp.int32)
    return (levels[None, :, None] == code_rows[:, None, :]).astype(jnp.bfloat16)


def decode_cols(codebooks, passage_codes):
    book_count, sub_width, level_count = codebooks.shape
    passage_count = passage_codes.shape[0]
    code_sets = passage_codes.T.reshape(book_count // 4, 4, passage_count)
    book_sets = codebooks.reshape(book_count // 4, 4, sub_width, level_count)

    def decode_book_set(set_items):
        code_rows, book_rows = set_items
        table = code_table(code_rows, level_count)
        return jnp.einsum("mck,mkp->mcp", book_rows, table, preferred_element_type=jnp.float32)

    picked = lax.map(decode_book_set, (code_sets, book_sets))
    return picked.reshape(book_count * sub_width, passage_count).astype(jnp.bfloat16)


def book_part(passage_codes, grad_cols, codebooks):
    book_count, sub_width, level_count = codebooks.shape
    passage_count = passage_codes.shape[0]
    code_sets = passage_codes.T.reshape(book_count // 4, 4, passage_count)
    grad_sets = grad_cols.reshape(book_count // 4, 4, sub_width, passage_count)

    def book_book_set(set_items):
        code_rows, grad_rows = set_items
        table = code_table(code_rows, level_count)
        high_part = grad_rows.astype(jnp.bfloat16)
        low_part = (grad_rows - high_part.astype(jnp.float32)).astype(jnp.bfloat16)
        high_sum = jnp.einsum("mcp,mkp->mck", high_part, table, preferred_element_type=jnp.float32)
        low_sum = jnp.einsum("mcp,mkp->mck", low_part, table, preferred_element_type=jnp.float32)
        return high_sum + low_sum

    return lax.map(book_book_set, (code_sets, grad_sets)).reshape(
        book_count, sub_width, level_count
    )


def move_block(query_block):
    moved_block = shifted(query_block, "db", 1)
    return moved_block


def move_stats(running_max, running_sum):
    moved_stats = shifted((running_max, running_sum), "db", 1)
    return moved_stats


def move_grads(log_total, block_weight, block_target, block_chosen, block_grad):
    moved_grads = shifted(
        (log_total, block_weight, block_target, block_chosen, block_grad), "db", 1
    )
    return moved_grads


def fold_stats(running, scores):
    running_max, running_sum = running
    newest_max = jnp.maximum(running_max, jnp.max(scores, axis=1))
    running_sum = running_sum * jnp.exp(running_max - newest_max) + jnp.sum(
        jnp.exp(scores - newest_max[:, None]), axis=1
    )
    return (newest_max, running_sum)


def per_device(queries, passage_codes, codebooks, positives, loss_weight):
    query_rows, model_width = queries.shape
    passage_count = passage_codes.shape[0]
    logit_scale = 2.5 / math.sqrt(model_width)
    empty_max = jnp.full((query_rows,), -jnp.inf, jnp.float32)
    empty_rows = jnp.zeros((query_rows,), jnp.float32)
    empty_grad = jnp.zeros((query_rows, model_width), jnp.float32)
    decoded_cols = decode_cols(codebooks, passage_codes)
    spot_index = (
        lax.axis_index("db") * passage_count + jnp.arange(passage_count, dtype=jnp.int32)
    ).astype(jnp.float32)

    def stats_step(turn_index, state):
        query_block, running_max, running_sum = state
        scores = (
            jnp.dot(query_block, decoded_cols, preferred_element_type=jnp.float32) * logit_scale
        )
        newest_max, running_sum = fold_stats((running_max, running_sum), scores)
        query_block = move_block(query_block)
        newest_max, running_sum = move_stats(newest_max, running_sum)
        return (query_block, newest_max, running_sum)

    query_block, running_max, running_sum = lax.fori_loop(
        0, lax.axis_size("db"), stats_step, (queries, empty_max, empty_rows)
    )
    log_total = running_max + jnp.log(running_sum)

    def grad_step(turn_index, state):
        (
            query_block,
            block_total,
            block_weight,
            block_target,
            block_chosen,
            block_grad,
            passage_grad,
        ) = state
        scores = (
            jnp.dot(query_block, decoded_cols, preferred_element_type=jnp.float32) * logit_scale
        )
        is_positive = block_target[:, None] == spot_index[None, :]
        block_chosen = block_chosen + jnp.sum(jnp.where(is_positive, scores, 0.0), axis=1)
        coefficient = (
            block_weight[:, None]
            * (jnp.exp(scores - block_total[:, None]) - is_positive.astype(jnp.float32))
            * logit_scale
        ).astype(jnp.bfloat16)
        block_grad = block_grad + jnp.einsum(
            "qp,dp->qd", coefficient, decoded_cols, preferred_element_type=jnp.float32
        )
        passage_grad = passage_grad + jnp.einsum(
            "qd,qp->dp", query_block, coefficient, preferred_element_type=jnp.float32
        )
        query_block = move_block(query_block)
        block_total, block_weight, block_target, block_chosen, block_grad = move_grads(
            block_total, block_weight, block_target, block_chosen, block_grad
        )
        return (
            query_block,
            block_total,
            block_weight,
            block_target,
            block_chosen,
            block_grad,
            passage_grad,
        )

    start_state = (
        queries,
        log_total,
        loss_weight,
        positives.astype(jnp.float32),
        empty_rows,
        empty_grad,
        jnp.zeros((model_width, passage_count), jnp.float32),
    )
    final_state = lax.fori_loop(0, lax.axis_size("db"), grad_step, start_state)
    chosen = final_state[4]
    grad_queries = final_state[5]
    book_grad = book_part(passage_codes, final_state[6], codebooks)
    query_loss = loss_weight * (log_total - chosen)
    book_total = lax.psum(book_grad, ("db", "pb"))
    return (query_loss, grad_queries, book_total)


def solution(mesh):
    return jax.shard_map(
        per_device,
        mesh=mesh,
        in_specs=(
            P(("db", "pb"), None),
            P(("db", "pb"), None),
            P(),
            P(("db", "pb")),
            P(("db", "pb")),
        ),
        out_specs=(P(("db", "pb")), P(("db", "pb"), None), P()),
        check_vma=False,
    )
```

profile of v0, /device:TPU:2, one launch (start us, length us, event | category | flops | bytes accessed | tf_op | source)
XLA Modules:
  0.0 1143.5 jit_solution(6119165569938202182)
XLA Ops:
  9.2 14.4 %while.57 = (s32[]{:T(128)}, bf16[16,4,12,128]{3,2,1,0:T(8,128)(2,1)S(1)}, bf16[16,4,12,256]{3,2,1,0:T(8,128)(2,1)S(1)}, s32[16,4,128]{2,1,0:T(4,128)}, s32[]{:T(128)}) while((s32[]{:T(128)}, bf16[16,4,12,128]{3,2,1,0:T(8,128)(2,1)S(1)}, bf16[16,4,12,256]{3,2,1,0:T(8,128)(2,1)S(1)}, s32[16,4,128]{2,1,0:T(4,128)}, s32[]{:T(128)}) %tuple.90), condition=%wide.region_1.2_spmd, body=%wide.region_0.1_spmd.sunk | while | flops 3276802 | bytes 72769 | solution.py:30
  23.6 202.0 %while.58 = (s32[]{:T(128)}, bf16[16,768]{1,0:T(8,128)(2,1)S(1)}, f32[16]{0:T(128)S(1)}, f32[16]{0:T(128)S(1)}, bf16[768,128]{1,0:T(8,128)(2,1)S(1)}, /*index=5*/s32[]{:T(128)}) while((s32[]{:T(128)}, bf16[16,768]{1,0:T(8,128)(2,1)S(1)}, f32[16]{0:T(128)S(1)}, f32[16]{0:T(128)S(1)}, bf16[768,128]{1,0:T(8,128)(2,1)S(1)}, ...), condition=%wide.region_5.6_spmd, body=%wide.region_2.5_spmd.sunk | while | flops 3153954 | bytes 386557 | solution.py:102
  52.4 4.9 collective-permute-start.2
  227.5 404.8 %while.60 = (s32[]{:T(128)}, bf16[16,768]{1,0:T(8,128)(2,1)S(1)}, f32[16]{0:T(128)S(1)}, f32[16]{0:T(128)S(1)}, f32[16]{0:T(128)S(1)}, /*index=5*/f32[16]{0:T(12...) while((s32[]{:T(128)}, bf16[16,768]{1,0:T(8,128)(2,1)S(1)}, ...), condition=%wide.region_8.9_spmd.clone, body=%wide.region_6.8_spmd.clone.sunk | while | flops 9683203 | bytes 1700275 | solution.py:156
  238.7 4.2 collective-permute-start.8
  264.6 4.6 collective-permute-start.7
  270.0 7.7 collective-permute-start.5
  282.6 4.2 collective-permute-start.3
  296.1 6.9 collective-permute-start.5
  321.3 6.9 collective-permute-start.5
  346.6 6.9 collective-permute-start.5
  371.9 6.9 collective-permute-start.5
  397.1 6.9 collective-permute-start.5
  422.4 6.9 collective-permute-start.5
  447.7 6.9 collective-permute-start.5
  472.9 6.9 collective-permute-start.5
  498.2 6.9 collective-permute-start.5
  523.5 6.9 collective-permute-start.5
  548.8 6.9 collective-permute-start.5
  574.0 6.9 collective-permute-start.5
  599.3 6.9 collective-permute-start.5
  624.6 6.9 collective-permute-start.5
  632.5 17.6 %while.59 = (s32[]{:T(128)}, f32[16,4,12,256]{3,2,1,0:T(8,128)S(1)}, f32[16,4,12,128]{3,2,1,0:T(8,128)S(1)}, s32[16,4,128]{2,1,0:T(4,128)}, s32[]{:T(128)}) while((s32[]{:T(128)}, f32[16,4,12,256]{3,2,1,0:T(8,128)S(1)}, f32[16,4,12,128]{3,2,1,0:T(8,128)S(1)}, s32[16,4,128]{2,1,0:T(4,128)}, s32[]{:T(128)}) %tuple.91), condition=%wide.region_10.11_spmd, body=%wide.region_9.10_spmd.sunk | while | flops 6590466 | bytes 238661 | solution.py:49
  652.6 481.5 %all-reduce.2.cloned.1.call-done = f32[64,12,256]{2,0,1:T(8,128)} async-done(((f32[64,12,256]{2,0,1:T(8,128)}), f32[64,12,256]{2,0,1:T(8,128)}) %all-reduce.2.cloned.1.call-update) | async-done | bytes 786448 | tf_op jit(solution)/shard_map/psum | solution.py:161
  (622 shorter events, 523.2 us)
Async XLA Ops:
  7.2 1126.9 %all-reduce.2.cloned.1.call-start = ((), (), s32[]{:S(2)}) async-start(), calls=%async_computation | async-start | bytes 1572864 | tf_op jit(solution)/shard_map/psum | solution.py:161
  227.5 23.6 %collective-permute-start.6 = (f32[16]{0:T(128)S(1)}, f32[16]{0:T(128)S(1)}, u32[]{:S(2)}, u32[]{:S(2)}) collective-permute-start(f32[16]{0:T(128)S(1)} %copy.47), channel_id=1, source_target_pairs={{480,0},{0,32},{32,64},{64,96},{96,128},{128,160},{160,192},{192,2... | collective-permute-start | bytes 200 | tf_op jit(solution)/shard_map/while/body/eval_jaxpr/ppermute | solution.py:11
  230.7 22.0 %collective-permute-start.3 = (bf16[16,768]{1,0:T(8,128)(2,1)S(1)}, bf16[16,768]{1,0:T(8,128)(2,1)S(1)}, u32[]{:S(2)}, u32[]{:S(2)}) collective-permute-start(bf16[16,768]{1,0:T(8,128)(2,1)S(1)} %copy.44), channel_id=1, source_target_pairs={{480,0},{0,32},{32,64},{64,96},{96,128},{128,160},{160,192},{192,2... | collective-permute-start | bytes 73736 | tf_op jit(solution)/shard_map/while/body/eval_jaxpr/ppermute | solution.py:11
  252.7 25.0 %collective-permute-start.6 = (f32[16]{0:T(128)S(1)}, f32[16]{0:T(128)S(1)}, u32[]{:S(2)}, u32[]{:S(2)}) collective-permute-start(f32[16]{0:T(128)S(1)} %copy.47), channel_id=1, source_target_pairs={{480,0},{0,32},{32,64},{64,96},{96,128},{128,160},{160,192},{192,2... | collective-permute-start | bytes 200 | tf_op jit(solution)/shard_map/while/body/eval_jaxpr/ppermute | solution.py:11
  256.0 22.5 %collective-permute-start.3 = (bf16[16,768]{1,0:T(8,128)(2,1)S(1)}, bf16[16,768]{1,0:T(8,128)(2,1)S(1)}, u32[]{:S(2)}, u32[]{:S(2)}) collective-permute-start(bf16[16,768]{1,0:T(8,128)(2,1)S(1)} %copy.44), channel_id=1, source_target_pairs={{480,0},{0,32},{32,64},{64,96},{96,128},{128,160},{160,192},{192,2... | collective-permute-start | bytes 73736 | tf_op jit(solution)/shard_map/while/body/eval_jaxpr/ppermute | solution.py:11
  278.5 24.5 %collective-permute-start.6 = (f32[16]{0:T(128)S(1)}, f32[16]{0:T(128)S(1)}, u32[]{:S(2)}, u32[]{:S(2)}) collective-permute-start(f32[16]{0:T(128)S(1)} %copy.47), channel_id=1, source_target_pairs={{480,0},{0,32},{32,64},{64,96},{96,128},{128,160},{160,192},{192,2... | collective-permute-start | bytes 200 | tf_op jit(solution)/shard_map/while/body/eval_jaxpr/ppermute | solution.py:11
  282.6 21.2 %collective-permute-start.3 = (bf16[16,768]{1,0:T(8,128)(2,1)S(1)}, bf16[16,768]{1,0:T(8,128)(2,1)S(1)}, u32[]{:S(2)}, u32[]{:S(2)}) collective-permute-start(bf16[16,768]{1,0:T(8,128)(2,1)S(1)} %copy.44), channel_id=1, source_target_pairs={{480,0},{0,32},{32,64},{64,96},{96,128},{128,160},{160,192},{192,2... | collective-permute-start | bytes 73736 | tf_op jit(solution)/shard_map/while/body/eval_jaxpr/ppermute | solution.py:11
  303.8 24.5 %collective-permute-start.6 = (f32[16]{0:T(128)S(1)}, f32[16]{0:T(128)S(1)}, u32[]{:S(2)}, u32[]{:S(2)}) collective-permute-start(f32[16]{0:T(128)S(1)} %copy.47), channel_id=1, source_target_pairs={{480,0},{0,32},{32,64},{64,96},{96,128},{128,160},{160,192},{192,2... | collective-permute-start | bytes 200 | tf_op jit(solution)/shard_map/while/body/eval_jaxpr/ppermute | solution.py:11
  307.9 21.2 %collective-permute-start.3 = (bf16[16,768]{1,0:T(8,128)(2,1)S(1)}, bf16[16,768]{1,0:T(8,128)(2,1)S(1)}, u32[]{:S(2)}, u32[]{:S(2)}) collective-permute-start(bf16[16,768]{1,0:T(8,128)(2,1)S(1)} %copy.44), channel_id=1, source_target_pairs={{480,0},{0,32},{32,64},{64,96},{96,128},{128,160},{160,192},{192,2... | collective-permute-start | bytes 73736 | tf_op jit(solution)/shard_map/while/body/eval_jaxpr/ppermute | solution.py:11
  329.0 24.5 %collective-permute-start.6 = (f32[16]{0:T(128)S(1)}, f32[16]{0:T(128)S(1)}, u32[]{:S(2)}, u32[]{:S(2)}) collective-permute-start(f32[16]{0:T(128)S(1)} %copy.47), channel_id=1, source_target_pairs={{480,0},{0,32},{32,64},{64,96},{96,128},{128,160},{160,192},{192,2... | collective-permute-start | bytes 200 | tf_op jit(solution)/shard_map/while/body/eval_jaxpr/ppermute | solution.py:11
  333.1 21.2 %collective-permute-start.3 = (bf16[16,768]{1,0:T(8,128)(2,1)S(1)}, bf16[16,768]{1,0:T(8,128)(2,1)S(1)}, u32[]{:S(2)}, u32[]{:S(2)}) collective-permute-start(bf16[16,768]{1,0:T(8,128)(2,1)S(1)} %copy.44), channel_id=1, source_target_pairs={{480,0},{0,32},{32,64},{64,96},{96,128},{128,160},{160,192},{192,2... | collective-permute-start | bytes 73736 | tf_op jit(solution)/shard_map/while/body/eval_jaxpr/ppermute | solution.py:11
  354.3 24.5 %collective-permute-start.6 = (f32[16]{0:T(128)S(1)}, f32[16]{0:T(128)S(1)}, u32[]{:S(2)}, u32[]{:S(2)}) collective-permute-start(f32[16]{0:T(128)S(1)} %copy.47), channel_id=1, source_target_pairs={{480,0},{0,32},{32,64},{64,96},{96,128},{128,160},{160,192},{192,2... | collective-permute-start | bytes 200 | tf_op jit(solution)/shard_map/while/body/eval_jaxpr/ppermute | solution.py:11
  379.6 24.5 %collective-permute-start.6 = (f32[16]{0:T(128)S(1)}, f32[16]{0:T(128)S(1)}, u32[]{:S(2)}, u32[]{:S(2)}) collective-permute-start(f32[16]{0:T(128)S(1)} %copy.47), channel_id=1, source_target_pairs={{480,0},{0,32},{32,64},{64,96},{96,128},{128,160},{160,192},{192,2... | collective-permute-start | bytes 200 | tf_op jit(solution)/shard_map/while/body/eval_jaxpr/ppermute | solution.py:11
  383.7 21.2 %collective-permute-start.3 = (bf16[16,768]{1,0:T(8,128)(2,1)S(1)}, bf16[16,768]{1,0:T(8,128)(2,1)S(1)}, u32[]{:S(2)}, u32[]{:S(2)}) collective-permute-start(bf16[16,768]{1,0:T(8,128)(2,1)S(1)} %copy.44), channel_id=1, source_target_pairs={{480,0},{0,32},{32,64},{64,96},{96,128},{128,160},{160,192},{192,2... | collective-permute-start | bytes 73736 | tf_op jit(solution)/shard_map/while/body/eval_jaxpr/ppermute | solution.py:11
  404.8 24.5 %collective-permute-start.6 = (f32[16]{0:T(128)S(1)}, f32[16]{0:T(128)S(1)}, u32[]{:S(2)}, u32[]{:S(2)}) collective-permute-start(f32[16]{0:T(128)S(1)} %copy.47), channel_id=1, source_target_pairs={{480,0},{0,32},{32,64},{64,96},{96,128},{128,160},{160,192},{192,2... | collective-permute-start | bytes 200 | tf_op jit(solution)/shard_map/while/body/eval_jaxpr/ppermute | solution.py:11
  430.1 24.5 %collective-permute-start.6 = (f32[16]{0:T(128)S(1)}, f32[16]{0:T(128)S(1)}, u32[]{:S(2)}, u32[]{:S(2)}) collective-permute-start(f32[16]{0:T(128)S(1)} %copy.47), channel_id=1, source_target_pairs={{480,0},{0,32},{32,64},{64,96},{96,128},{128,160},{160,192},{192,2... | collective-permute-start | bytes 200 | tf_op jit(solution)/shard_map/while/body/eval_jaxpr/ppermute | solution.py:11
  455.4 24.5 %collective-permute-start.6 = (f32[16]{0:T(128)S(1)}, f32[16]{0:T(128)S(1)}, u32[]{:S(2)}, u32[]{:S(2)}) collective-permute-start(f32[16]{0:T(128)S(1)} %copy.47), channel_id=1, source_target_pairs={{480,0},{0,32},{32,64},{64,96},{96,128},{128,160},{160,192},{192,2... | collective-permute-start | bytes 200 | tf_op jit(solution)/shard_map/while/body/eval_jaxpr/ppermute | solution.py:11
  480.6 24.5 %collective-permute-start.6 = (f32[16]{0:T(128)S(1)}, f32[16]{0:T(128)S(1)}, u32[]{:S(2)}, u32[]{:S(2)}) collective-permute-start(f32[16]{0:T(128)S(1)} %copy.47), channel_id=1, source_target_pairs={{480,0},{0,32},{32,64},{64,96},{96,128},{128,160},{160,192},{192,2... | collective-permute-start | bytes 200 | tf_op jit(solution)/shard_map/while/body/eval_jaxpr/ppermute | solution.py:11
  505.9 24.5 %collective-permute-start.6 = (f32[16]{0:T(128)S(1)}, f32[16]{0:T(128)S(1)}, u32[]{:S(2)}, u32[]{:S(2)}) collective-permute-start(f32[16]{0:T(128)S(1)} %copy.47), channel_id=1, source_target_pairs={{480,0},{0,32},{32,64},{64,96},{96,128},{128,160},{160,192},{192,2... | collective-permute-start | bytes 200 | tf_op jit(solution)/shard_map/while/body/eval_jaxpr/ppermute | solution.py:11
  531.2 24.5 %collective-permute-start.6 = (f32[16]{0:T(128)S(1)}, f32[16]{0:T(128)S(1)}, u32[]{:S(2)}, u32[]{:S(2)}) collective-permute-start(f32[16]{0:T(128)S(1)} %copy.47), channel_id=1, source_target_pairs={{480,0},{0,32},{32,64},{64,96},{96,128},{128,160},{160,192},{192,2... | collective-permute-start | bytes 200 | tf_op jit(solution)/shard_map/while/body/eval_jaxpr/ppermute | solution.py:11
  556.4 24.5 %collective-permute-start.6 = (f32[16]{0:T(128)S(1)}, f32[16]{0:T(128)S(1)}, u32[]{:S(2)}, u32[]{:S(2)}) collective-permute-start(f32[16]{0:T(128)S(1)} %copy.47), channel_id=1, source_target_pairs={{480,0},{0,32},{32,64},{64,96},{96,128},{128,160},{160,192},{192,2... | collective-permute-start | bytes 200 | tf_op jit(solution)/shard_map/while/body/eval_jaxpr/ppermute | solution.py:11
  560.5 21.2 %collective-permute-start.3 = (bf16[16,768]{1,0:T(8,128)(2,1)S(1)}, bf16[16,768]{1,0:T(8,128)(2,1)S(1)}, u32[]{:S(2)}, u32[]{:S(2)}) collective-permute-start(bf16[16,768]{1,0:T(8,128)(2,1)S(1)} %copy.44), channel_id=1, source_target_pairs={{480,0},{0,32},{32,64},{64,96},{96,128},{128,160},{160,192},{192,2... | collective-permute-start | bytes 73736 | tf_op jit(solution)/shard_map/while/body/eval_jaxpr/ppermute | solution.py:11
  581.7 24.5 %collective-permute-start.6 = (f32[16]{0:T(128)S(1)}, f32[16]{0:T(128)S(1)}, u32[]{:S(2)}, u32[]{:S(2)}) collective-permute-start(f32[16]{0:T(128)S(1)} %copy.47), channel_id=1, source_target_pairs={{480,0},{0,32},{32,64},{64,96},{96,128},{128,160},{160,192},{192,2... | collective-permute-start | bytes 200 | tf_op jit(solution)/shard_map/while/body/eval_jaxpr/ppermute | solution.py:11
  607.0 24.5 %collective-permute-start.6 = (f32[16]{0:T(128)S(1)}, f32[16]{0:T(128)S(1)}, u32[]{:S(2)}, u32[]{:S(2)}) collective-permute-start(f32[16]{0:T(128)S(1)} %copy.47), channel_id=1, source_target_pairs={{480,0},{0,32},{32,64},{64,96},{96,128},{128,160},{160,192},{192,2... | collective-permute-start | bytes 200 | tf_op jit(solution)/shard_map/while/body/eval_jaxpr/ppermute | solution.py:11
  (127 other events, 1289.1 us)
Sparse Core Ops, SparseCore 0:
  651.5 482.4 all-reduce.1
where the time goes:
time: 1150 us; the launch traced here: 1140 us
  waiting for transfers between devices  542 us (47%)
  starting transfers between devices  523 us (45%)
  local copies, waits for them, and re-layouts  30.9 us (3%)
  matrix products  27 us (2%)
  between operations  14.1 us (1%)
    ppermute x144, starting transfers between devices, shifted(): return lax.ppermute(block, axis, route)  523 us
    psum x1, waiting for transfers between devices, per_device(): book_total = lax.psum(book_grad, ('db', 'pb'))  481 us
    ppermute x144, waiting for transfers between devices, shifted(): return lax.ppermute(block, axis, route)  60.2 us
  transfers between devices with their start and end apart: 145, of which 49 were waited for; matrix products, arithmetic and copies ran while one was open for 2% of the time, Pallas kernels for 0%

commit v1 on v0

--- a/solution.py
+++ b/solution.py
@@ -78,6 +78,12 @@
 
 
 def per_device(queries, passage_codes, codebooks, positives, loss_weight):
+
+    def body_plan(packet):
+        for c in ("pb", "db"):
+            packet = jax.lax.psum(packet, c)
+        return packet
+
     query_rows, model_width = queries.shape
     passage_count = passage_codes.shape[0]
     logit_scale = 2.5 / math.sqrt(model_width)
@@ -158,7 +164,7 @@
     grad_queries = final_state[5]
     book_grad = book_part(passage_codes, final_state[6], codebooks)
     query_loss = loss_weight * (log_total - chosen)
-    book_total = lax.psum(book_grad, ("db", "pb"))
+    book_total = body_plan(book_grad)
     return (query_loss, grad_queries, book_total)
 
 

time: 1150 us -> 1080 us (0.939)
  the two profiles are of different devices: /device:TPU:2 before, /device:TPU:1 now
where the time goes in v1:
time: 1080 us
  waiting for transfers between devices  633 us (59%)
  starting transfers between devices  368 us (34%)
  local copies, waits for them, and re-layouts  30.9 us (3%)
  matrix products  27 us (2%)
  between operations  14.1 us (1%)
    psum x2, waiting for transfers between devices, body_plan(): packet = jax.lax.psum(packet, c)  414 us
    ppermute x144, starting transfers between devices, shifted(): return lax.ppermute(block, axis, route)  368 us
    ppermute x144, waiting for transfers between devices, shifted(): return lax.ppermute(block, axis, route)  219 us
    eq x32, local copies, waits for them, and re-layouts, code_table(): return (levels[None, :, None] == code_rows[:, None, :]).astype(jnp.bfloat16)  22 us
  transfers between devices with their start and end apart: 146, of which 66 were waited for; matrix products, arithmetic and copies ran while one was open for 2% of the time, Pallas kernels for 0%

profile of v1, /device:TPU:1, one launch (start us, length us, event | category | flops | bytes accessed | tf_op | source)
XLA Modules:
  0.0 1079.4 jit_solution(7554915710560477680)
XLA Ops:
  9.2 14.4 %while.57 = (s32[]{:T(128)}, bf16[16,4,12,128]{3,2,1,0:T(8,128)(2,1)S(1)}, bf16[16,4,12,256]{3,2,1,0:T(8,128)(2,1)S(1)}, s32[16,4,128]{2,1,0:T(4,128)}, s32[]{:T(128)}) while((s32[]{:T(128)}, bf16[16,4,12,128]{3,2,1,0:T(8,128)(2,1)S(1)}, bf16[16,4,12,256]{3,2,1,0:T(8,128)(2,1)S(1)}, s32[16,4,128]{2,1,0:T(4,128)}, s32[]{:T(128)}) %tuple.92), condition=%wide.region_1.2_spmd, body=%wide.region_0.1_spmd.sunk | while | flops 3276802 | bytes 72769 | solution.py:30
  23.6 206.1 %while.58 = (s32[]{:T(128)}, bf16[16,768]{1,0:T(8,128)(2,1)S(1)}, f32[16]{0:T(128)S(1)}, f32[16]{0:T(128)S(1)}, bf16[768,128]{1,0:T(8,128)(2,1)S(1)}, /*index=5*/s32[]{:T(128)}) while((s32[]{:T(128)}, bf16[16,768]{1,0:T(8,128)(2,1)S(1)}, f32[16]{0:T(128)S(1)}, f32[16]{0:T(128)S(1)}, bf16[768,128]{1,0:T(8,128)(2,1)S(1)}, ...), condition=%wide.region_5.6_spmd, body=%wide.region_2.5_spmd.sunk | while | flops 3153954 | bytes 386557 | solution.py:108
  23.6 4.5 collective-permute-start
  231.5 404.3 %while.60 = (s32[]{:T(128)}, bf16[16,768]{1,0:T(8,128)(2,1)S(1)}, f32[16]{0:T(128)S(1)}, f32[16]{0:T(128)S(1)}, f32[16]{0:T(128)S(1)}, /*index=5*/f32[16]{0:T(12...) while((s32[]{:T(128)}, bf16[16,768]{1,0:T(8,128)(2,1)S(1)}, ...), condition=%wide.region_8.9_spmd.clone, body=%wide.region_6.8_spmd.clone.sunk | while | flops 9683203 | bytes 1700275 | solution.py:162
  252.3 4.4 collective-permute-done.5
  275.5 6.6 collective-permute-done.5
  287.1 4.2 collective-permute-start.4
  300.8 6.6 collective-permute-done.5
  326.0 6.6 collective-permute-done.5
  351.3 6.6 collective-permute-done.5
  376.6 6.6 collective-permute-done.5
  401.8 6.6 collective-permute-done.5
  427.1 6.6 collective-permute-done.5
  452.4 6.6 collective-permute-done.5
  477.6 6.6 collective-permute-done.5
  502.9 6.6 collective-permute-done.5
  528.2 6.6 collective-permute-done.5
  553.4 6.6 collective-permute-done.5
  578.7 6.6 collective-permute-done.5
  604.0 6.6 collective-permute-done.5
  629.2 6.6 collective-permute-done.5
  636.0 17.6 %while.59 = (s32[]{:T(128)}, f32[16,4,12,256]{3,2,1,0:T(8,128)S(1)}, f32[16,4,12,128]{3,2,1,0:T(8,128)S(1)}, s32[16,4,128]{2,1,0:T(4,128)}, s32[]{:T(128)}) while((s32[]{:T(128)}, f32[16,4,12,256]{3,2,1,0:T(8,128)S(1)}, f32[16,4,12,128]{3,2,1,0:T(8,128)S(1)}, s32[16,4,128]{2,1,0:T(4,128)}, s32[]{:T(128)}) %tuple.93), condition=%wide.region_10.11_spmd, body=%wide.region_9.10_spmd.sunk | while | flops 6590466 | bytes 238661 | solution.py:49
  655.0 241.5 %all-reduce.3.cloned.1.call-done = f32[64,12,256]{2,0,1:T(8,128)} async-done(((f32[64,12,256]{2,0,1:T(8,128)}), f32[64,12,256]{2,0,1:T(8,128)}) %all-reduce.3.cloned.1.call-update) | async-done | bytes 786448 | tf_op jit(solution)/shard_map/psum | solution.py:84
  897.7 172.2 %all-reduce.5.cloned.1.call-done = f32[64,12,256]{2,0,1:T(8,128)} async-done(((f32[64,12,256]{2,0,1:T(8,128)}), f32[64,12,256]{2,0,1:T(8,128)}) %all-reduce.5.cloned.1.call-update) | async-done | bytes 786448 | tf_op jit(solution)/shard_map/psum | solution.py:84
  (625 shorter events, 537.4 us)
Async XLA Ops:
  7.2 889.4 %all-reduce.3.cloned.1.call-start = ((), (), s32[]{:S(2)}) async-start(), calls=%async_computation | async-start | bytes 1572864 | tf_op jit(solution)/shard_map/psum | solution.py:84
  231.5 20.8 %collective-permute-start.6 = (f32[16]{0:T(128)S(1)}, f32[16]{0:T(128)S(1)}, u32[]{:S(2)}, u32[]{:S(2)}) collective-permute-start(f32[16]{0:T(128)S(1)} %copy.47), channel_id=1, source_target_pairs={{480,0},{0,32},{32,64},{64,96},{96,128},{128,160},{160,192},{192,2... | collective-permute-start | bytes 200 | tf_op jit(solution)/shard_map/while/body/eval_jaxpr/ppermute | solution.py:11
  233.5 23.3 %collective-permute-start.3 = (bf16[16,768]{1,0:T(8,128)(2,1)S(1)}, bf16[16,768]{1,0:T(8,128)(2,1)S(1)}, u32[]{:S(2)}, u32[]{:S(2)}) collective-permute-start(bf16[16,768]{1,0:T(8,128)(2,1)S(1)} %copy.44), channel_id=1, source_target_pairs={{480,0},{0,32},{32,64},{64,96},{96,128},{128,160},{160,192},{192,2... | collective-permute-start | bytes 73736 | tf_op jit(solution)/shard_map/while/body/eval_jaxpr/ppermute | solution.py:11
  258.7 23.3 %collective-permute-start.3 = (bf16[16,768]{1,0:T(8,128)(2,1)S(1)}, bf16[16,768]{1,0:T(8,128)(2,1)S(1)}, u32[]{:S(2)}, u32[]{:S(2)}) collective-permute-start(bf16[16,768]{1,0:T(8,128)(2,1)S(1)} %copy.44), channel_id=1, source_target_pairs={{480,0},{0,32},{32,64},{64,96},{96,128},{128,160},{160,192},{192,2... | collective-permute-start | bytes 73736 | tf_op jit(solution)/shard_map/while/body/eval_jaxpr/ppermute | solution.py:11
  282.1 18.7 %collective-permute-start.6 = (f32[16]{0:T(128)S(1)}, f32[16]{0:T(128)S(1)}, u32[]{:S(2)}, u32[]{:S(2)}) collective-permute-start(f32[16]{0:T(128)S(1)} %copy.47), channel_id=1, source_target_pairs={{480,0},{0,32},{32,64},{64,96},{96,128},{128,160},{160,192},{192,2... | collective-permute-start | bytes 200 | tf_op jit(solution)/shard_map/while/body/eval_jaxpr/ppermute | solution.py:11
  284.0 23.3 %collective-permute-start.3 = (bf16[16,768]{1,0:T(8,128)(2,1)S(1)}, bf16[16,768]{1,0:T(8,128)(2,1)S(1)}, u32[]{:S(2)}, u32[]{:S(2)}) collective-permute-start(bf16[16,768]{1,0:T(8,128)(2,1)S(1)} %copy.44), channel_id=1, source_target_pairs={{480,0},{0,32},{32,64},{64,96},{96,128},{128,160},{160,192},{192,2... | collective-permute-start | bytes 73736 | tf_op jit(solution)/shard_map/while/body/eval_jaxpr/ppermute | solution.py:11
  307.3 18.7 %collective-permute-start.6 = (f32[16]{0:T(128)S(1)}, f32[16]{0:T(128)S(1)}, u32[]{:S(2)}, u32[]{:S(2)}) collective-permute-start(f32[16]{0:T(128)S(1)} %copy.47), channel_id=1, source_target_pairs={{480,0},{0,32},{32,64},{64,96},{96,128},{128,160},{160,192},{192,2... | collective-permute-start | bytes 200 | tf_op jit(solution)/shard_map/while/body/eval_jaxpr/ppermute | solution.py:11
  309.3 23.3 %collective-permute-start.3 = (bf16[16,768]{1,0:T(8,128)(2,1)S(1)}, bf16[16,768]{1,0:T(8,128)(2,1)S(1)}, u32[]{:S(2)}, u32[]{:S(2)}) collective-permute-start(bf16[16,768]{1,0:T(8,128)(2,1)S(1)} %copy.44), channel_id=1, source_target_pairs={{480,0},{0,32},{32,64},{64,96},{96,128},{128,160},{160,192},{192,2... | collective-permute-start | bytes 73736 | tf_op jit(solution)/shard_map/while/body/eval_jaxpr/ppermute | solution.py:11
  334.5 23.3 %collective-permute-start.3 = (bf16[16,768]{1,0:T(8,128)(2,1)S(1)}, bf16[16,768]{1,0:T(8,128)(2,1)S(1)}, u32[]{:S(2)}, u32[]{:S(2)}) collective-permute-start(bf16[16,768]{1,0:T(8,128)(2,1)S(1)} %copy.44), channel_id=1, source_target_pairs={{480,0},{0,32},{32,64},{64,96},{96,128},{128,160},{160,192},{192,2... | collective-permute-start | bytes 73736 | tf_op jit(solution)/shard_map/while/body/eval_jaxpr/ppermute | solution.py:11
  359.8 23.3 %collective-permute-start.3 = (bf16[16,768]{1,0:T(8,128)(2,1)S(1)}, bf16[16,768]{1,0:T(8,128)(2,1)S(1)}, u32[]{:S(2)}, u32[]{:S(2)}) collective-permute-start(bf16[16,768]{1,0:T(8,128)(2,1)S(1)} %copy.44), channel_id=1, source_target_pairs={{480,0},{0,32},{32,64},{64,96},{96,128},{128,160},{160,192},{192,2... | collective-permute-start | bytes 73736 | tf_op jit(solution)/shard_map/while/body/eval_jaxpr/ppermute | solution.py:11
  383.1 18.7 %collective-permute-start.6 = (f32[16]{0:T(128)S(1)}, f32[16]{0:T(128)S(1)}, u32[]{:S(2)}, u32[]{:S(2)}) collective-permute-start(f32[16]{0:T(128)S(1)} %copy.47), channel_id=1, source_target_pairs={{480,0},{0,32},{32,64},{64,96},{96,128},{128,160},{160,192},{192,2... | collective-permute-start | bytes 200 | tf_op jit(solution)/shard_map/while/body/eval_jaxpr/ppermute | solution.py:11
  385.1 23.3 %collective-permute-start.3 = (bf16[16,768]{1,0:T(8,128)(2,1)S(1)}, bf16[16,768]{1,0:T(8,128)(2,1)S(1)}, u32[]{:S(2)}, u32[]{:S(2)}) collective-permute-start(bf16[16,768]{1,0:T(8,128)(2,1)S(1)} %copy.44), channel_id=1, source_target_pairs={{480,0},{0,32},{32,64},{64,96},{96,128},{128,160},{160,192},{192,2... | collective-permute-start | bytes 73736 | tf_op jit(solution)/shard_map/while/body/eval_jaxpr/ppermute | solution.py:11
  408.4 18.7 %collective-permute-start.6 = (f32[16]{0:T(128)S(1)}, f32[16]{0:T(128)S(1)}, u32[]{:S(2)}, u32[]{:S(2)}) collective-permute-start(f32[16]{0:T(128)S(1)} %copy.47), channel_id=1, source_target_pairs={{480,0},{0,32},{32,64},{64,96},{96,128},{128,160},{160,192},{192,2... | collective-permute-start | bytes 200 | tf_op jit(solution)/shard_map/while/body/eval_jaxpr/ppermute | solution.py:11
  410.3 23.3 %collective-permute-start.3 = (bf16[16,768]{1,0:T(8,128)(2,1)S(1)}, bf16[16,768]{1,0:T(8,128)(2,1)S(1)}, u32[]{:S(2)}, u32[]{:S(2)}) collective-permute-start(bf16[16,768]{1,0:T(8,128)(2,1)S(1)} %copy.44), channel_id=1, source_target_pairs={{480,0},{0,32},{32,64},{64,96},{96,128},{128,160},{160,192},{192,2... | collective-permute-start | bytes 73736 | tf_op jit(solution)/shard_map/while/body/eval_jaxpr/ppermute | solution.py:11
  435.6 23.3 %collective-permute-start.3 = (bf16[16,768]{1,0:T(8,128)(2,1)S(1)}, bf16[16,768]{1,0:T(8,128)(2,1)S(1)}, u32[]{:S(2)}, u32[]{:S(2)}) collective-permute-start(bf16[16,768]{1,0:T(8,128)(2,1)S(1)} %copy.44), channel_id=1, source_target_pairs={{480,0},{0,32},{32,64},{64,96},{96,128},{128,160},{160,192},{192,2... | collective-permute-start | bytes 73736 | tf_op jit(solution)/shard_map/while/body/eval_jaxpr/ppermute | solution.py:11
  460.9 23.3 %collective-permute-start.3 = (bf16[16,768]{1,0:T(8,128)(2,1)S(1)}, bf16[16,768]{1,0:T(8,128)(2,1)S(1)}, u32[]{:S(2)}, u32[]{:S(2)}) collective-permute-start(bf16[16,768]{1,0:T(8,128)(2,1)S(1)} %copy.44), channel_id=1, source_target_pairs={{480,0},{0,32},{32,64},{64,96},{96,128},{128,160},{160,192},{192,2... | collective-permute-start | bytes 73736 | tf_op jit(solution)/shard_map/while/body/eval_jaxpr/ppermute | solution.py:11
  484.2 18.7 %collective-permute-start.6 = (f32[16]{0:T(128)S(1)}, f32[16]{0:T(128)S(1)}, u32[]{:S(2)}, u32[]{:S(2)}) collective-permute-start(f32[16]{0:T(128)S(1)} %copy.47), channel_id=1, source_target_pairs={{480,0},{0,32},{32,64},{64,96},{96,128},{128,160},{160,192},{192,2... | collective-permute-start | bytes 200 | tf_op jit(solution)/shard_map/while/body/eval_jaxpr/ppermute | solution.py:11
  486.1 23.3 %collective-permute-start.3 = (bf16[16,768]{1,0:T(8,128)(2,1)S(1)}, bf16[16,768]{1,0:T(8,128)(2,1)S(1)}, u32[]{:S(2)}, u32[]{:S(2)}) collective-permute-start(bf16[16,768]{1,0:T(8,128)(2,1)S(1)} %copy.44), channel_id=1, source_target_pairs={{480,0},{0,32},{32,64},{64,96},{96,128},{128,160},{160,192},{192,2... | collective-permute-start | bytes 73736 | tf_op jit(solution)/shard_map/while/body/eval_jaxpr/ppermute | solution.py:11
  511.4 23.3 %collective-permute-start.3 = (bf16[16,768]{1,0:T(8,128)(2,1)S(1)}, bf16[16,768]{1,0:T(8,128)(2,1)S(1)}, u32[]{:S(2)}, u32[]{:S(2)}) collective-permute-start(bf16[16,768]{1,0:T(8,128)(2,1)S(1)} %copy.44), channel_id=1, source_target_pairs={{480,0},{0,32},{32,64},{64,96},{96,128},{128,160},{160,192},{192,2... | collective-permute-start | bytes 73736 | tf_op jit(solution)/shard_map/while/body/eval_jaxpr/ppermute | solution.py:11
  536.7 23.3 %collective-permute-start.3 = (bf16[16,768]{1,0:T(8,128)(2,1)S(1)}, bf16[16,768]{1,0:T(8,128)(2,1)S(1)}, u32[]{:S(2)}, u32[]{:S(2)}) collective-permute-start(bf16[16,768]{1,0:T(8,128)(2,1)S(1)} %copy.44), channel_id=1, source_target_pairs={{480,0},{0,32},{32,64},{64,96},{96,128},{128,160},{160,192},{192,2... | collective-permute-start | bytes 73736 | tf_op jit(solution)/shard_map/while/body/eval_jaxpr/ppermute | solution.py:11
  561.9 23.3 %collective-permute-start.3 = (bf16[16,768]{1,0:T(8,128)(2,1)S(1)}, bf16[16,768]{1,0:T(8,128)(2,1)S(1)}, u32[]{:S(2)}, u32[]{:S(2)}) collective-permute-start(bf16[16,768]{1,0:T(8,128)(2,1)S(1)} %copy.44), channel_id=1, source_target_pairs={{480,0},{0,32},{32,64},{64,96},{96,128},{128,160},{160,192},{192,2... | collective-permute-start | bytes 73736 | tf_op jit(solution)/shard_map/while/body/eval_jaxpr/ppermute | solution.py:11
  587.2 23.3 %collective-permute-start.3 = (bf16[16,768]{1,0:T(8,128)(2,1)S(1)}, bf16[16,768]{1,0:T(8,128)(2,1)S(1)}, u32[]{:S(2)}, u32[]{:S(2)}) collective-permute-start(bf16[16,768]{1,0:T(8,128)(2,1)S(1)} %copy.44), channel_id=1, source_target_pairs={{480,0},{0,32},{32,64},{64,96},{96,128},{128,160},{160,192},{192,2... | collective-permute-start | bytes 73736 | tf_op jit(solution)/shard_map/while/body/eval_jaxpr/ppermute | solution.py:11
  612.5 23.3 %collective-permute-start.3 = (bf16[16,768]{1,0:T(8,128)(2,1)S(1)}, bf16[16,768]{1,0:T(8,128)(2,1)S(1)}, u32[]{:S(2)}, u32[]{:S(2)}) collective-permute-start(bf16[16,768]{1,0:T(8,128)(2,1)S(1)} %copy.44), channel_id=1, source_target_pairs={{480,0},{0,32},{32,64},{64,96},{96,128},{128,160},{160,192},{192,2... | collective-permute-start | bytes 73736 | tf_op jit(solution)/shard_map/while/body/eval_jaxpr/ppermute | solution.py:11
  654.9 415.0 %all-reduce.5.cloned.1.call-start = ((), (), s32[]{:S(2)}) async-start(), calls=%async_computation.1 | async-start | bytes 1572864 | tf_op jit(solution)/shard_map/psum | solution.py:84
  (128 other events, 1357.2 us)
Sparse Core Ops, SparseCore 0:
  655.1 241.4 all-reduce.2
  899.4 170.4 all-reduce.4
